TPU v7x, 128 devices: a whole 4x4x4 slice. The times are simulated.
128 devices in a mesh: dp: 16 (over x_lo, y, core), tensor: 8 (over x_hi, z).
Axes of the slice: x: 4 (x_hi: 2, x_lo: 2; x = x_hi * 2 + x_lo), y: 4, z: 4, core: 2. Of those that a mesh axis runs over, the one named last changes fastest.
Arguments:
- block_input: bfloat16 [32768, 768], P(('dp', 'tensor')), may hold values from -6 to 6
- w_value: bfloat16 [768, 768], replicated, may hold values from -0.21875 to 0.21875
- b_value: bfloat16 [768], replicated, may hold values from -2 to 2
- conv_kernel: bfloat16 [65, 768], replicated, may hold values from -0.75 to 0.75
- w_out: bfloat16 [768, 768], replicated, may hold values from -0.21875 to 0.21875
- b_out: bfloat16 [768], replicated, may hold values from -2 to 2
- gain_attn: bfloat16 [768], replicated, may hold values from 0.5 to 1.5
- shift_attn: bfloat16 [768], replicated, may hold values from -2 to 2
- w_up: bfloat16 [768, 3072], P(None, 'tensor'), may hold values from -0.21875 to 0.21875
- b_up: bfloat16 [3072], P('tensor'), may hold values from -2 to 2
- w_down: bfloat16 [3072, 768], P('tensor'), may hold values from -0.109375 to 0.109375
- b_down: bfloat16 [768], replicated, may hold values from -2 to 2
- gain_ffn: bfloat16 [768], replicated, may hold values from 0.5 to 1.5
- shift_ffn: bfloat16 [768], replicated, may hold values from -2 to 2
- query_codes: int32 [32768, 384], P(('dp', 'tensor')), may hold values from 0 to 255
- key_codes: int32 [32768, 384], P(('dp', 'tensor')), may hold values from 0 to 255
- key_live: int32 [32768], P(('dp', 'tensor')), may hold values 0 or 1
- seq_lengths: int32 [128, 4], P(('dp', 'tensor')), may hold values from 1 to 128, 256 in all within a row
- out_grad: bfloat16 [32768, 768], P(('dp', 'tensor')), may hold values from -6 to 6
Outputs:
- block_output: bfloat16 [32768, 768], P(('dp', 'tensor'))
- input_grad: float32 [32768, 768], P(('dp', 'tensor'))
- grad_w_value: float32 [768, 768], replicated
- grad_b_value: float32 [768], replicated
- grad_conv_kernel: float32 [65, 768], replicated
- grad_w_out: float32 [768, 768], replicated
- grad_b_out: float32 [768], replicated
- grad_gain_attn: float32 [768], replicated
- grad_shift_attn: float32 [768], replicated
- grad_w_up: float32 [768, 3072], P(None, 'tensor')
- grad_b_up: float32 [3072], P('tensor')
- grad_w_down: float32 [3072, 768], P('tensor')
- grad_b_down: float32 [768], replicated
- grad_gain_ffn: float32 [768], replicated
- grad_shift_ffn: float32 [768], replicated
Inputs may be any that keep to these rules, and one draw needn't show every extreme that they name: `seq_lengths`: each item's lengths sum to 256; the longest is 128. `key_live`: 1 marks a live key, 0 a padded one. `query_codes`: column h * 32 + s holds head h's code in hash set s. `key_codes`: column h * 32 + s holds head h's code in hash set s.
All inputs are finite; a program needn't handle non-finite values. No bound on the sum of `key_live` on one device may be relied on, other than what follows from the above.
Results may differ from a plain program's by a relative error of at most 0.02.
Values may be sent and summed in bfloat16 or wider, within the bound.
No kernel may reach another device: no remote copies, remote signals or barrier semaphores. Data moves between devices by JAX's collectives and lax.ppermute only.
A program may use at most 128 MiB of HBM per device.

v0:
```python
from functools import partial
import jax
import jax.numpy as jnp
from jax import lax
from jax.sharding import PartitionSpec as P

HEADS = 12
SETS = 32
BUCKETS = 256


def dot_last(former, latter):
    return lax.dot_general(
        former, latter, (((1,), (1,)), ((), ())), preferred_element_type=jnp.float32
    )


def dot_first(former, latter):
    return lax.dot_general(
        former, latter, (((0,), (0,)), ((), ())), preferred_element_type=jnp.float32
    )


def layer_norm(residual, gain_vec, shift_vec):
    average = jnp.mean(residual, axis=-1, keepdims=True)
    centred = residual - average
    variance = jnp.mean(centred * centred, axis=-1, keepdims=True)
    return centred * lax.rsqrt(variance + 1e-05) * gain_vec + shift_vec


def head_norm(mixed, head_count, head_dim):
    grouped = mixed.reshape(mixed.shape[0], head_count, head_dim)
    scaling = lax.rsqrt(jnp.mean(grouped * grouped, axis=-1, keepdims=True) + 1e-06)
    return (grouped * scaling).reshape(mixed.shape)


def gelu_exact(pre_act):
    return jax.nn.gelu(pre_act, approximate=False)


def depth_conv(values, kernel, segment):
    taps = kernel.shape[0]
    margin = taps // 2
    length = values.shape[0]
    padded = jnp.pad(values, ((margin, margin), (0, 0)))
    seg_padded = jnp.pad(segment, (margin, margin), constant_values=-1)
    running = jnp.zeros_like(values)
    for offset in range(taps):
        joined = (seg_padded[offset : offset + length] == segment).astype(jnp.float32)[:, None]
        running = running + padded[offset : offset + length] * joined * kernel[offset][None, :]
    return running


def conv_back(grad_out, values, kernel, segment):
    taps = kernel.shape[0]
    margin = taps // 2
    length = values.shape[0]
    padded = jnp.pad(values, ((margin, margin), (0, 0)))
    grad_padded = jnp.pad(grad_out, ((margin, margin), (0, 0)))
    seg_padded = jnp.pad(segment, (margin, margin), constant_values=-1)
    value_grad = jnp.zeros_like(values)
    tap_rows = []
    for offset in range(taps):
        joined = (seg_padded[offset : offset + length] == segment).astype(jnp.float32)[:, None]
        tap_rows.append(jnp.sum(grad_out * joined * padded[offset : offset + length], axis=0))
        mirror = 2 * margin - offset
        back_joined = (seg_padded[mirror : mirror + length] == segment).astype(jnp.float32)[:, None]
        value_grad = (
            value_grad
            + grad_padded[mirror : mirror + length] * back_joined * kernel[offset][None, :]
        )
    return (value_grad, jnp.stack(tap_rows, axis=0))


def body(
    block_input,
    w_value,
    b_value,
    conv_kernel,
    w_out,
    b_out,
    gain_attn,
    shift_attn,
    w_up,
    b_up,
    w_down,
    b_down,
    gain_ffn,
    shift_ffn,
    query_codes,
    key_codes,
    key_live,
    seq_lengths,
    out_grad,
):
    length = block_input.shape[0]
    model_width = block_input.shape[1]
    head_dim = model_width // HEADS
    live_keys = key_live.astype(jnp.float32)[:, None]
    seq_ends = jnp.cumsum(seq_lengths[0], dtype=jnp.int32)
    positions = jnp.arange(length, dtype=jnp.int32)
    segment = jnp.sum(
        (seq_ends[None, :] <= positions[:, None]).astype(jnp.int32), axis=1, dtype=jnp.int32
    )
    query_heads = query_codes.reshape(length, HEADS, SETS).transpose(1, 0, 2)
    key_heads = key_codes.reshape(length, HEADS, SETS).transpose(1, 0, 2)
    joined = (segment[:, None] == segment[None, :]).astype(jnp.float32)
    bucket_ids = jnp.arange(BUCKETS, dtype=jnp.int32)

    def head_counts(pair):
        query_set, key_set = pair
        query_hot = (
            (query_set[:, :, None] == bucket_ids[None, None, :])
            .astype(jnp.bfloat16)
            .reshape(length, SETS * BUCKETS)
        )
        key_hot = (
            (key_set[:, :, None] == bucket_ids[None, None, :])
            .astype(jnp.bfloat16)
            .reshape(length, SETS * BUCKETS)
        )
        counts = dot_last(query_hot, key_hot)
        return (counts * joined / SETS).astype(jnp.bfloat16)

    collide = lax.map(head_counts, (query_heads, key_heads))
    kernel_f = conv_kernel.astype(jnp.float32)
    value_pre = jnp.dot(block_input, w_value, preferred_element_type=jnp.float32) + b_value.astype(
        jnp.float32
    )
    values = value_pre.astype(jnp.bfloat16)
    masked = values.astype(jnp.float32) * live_keys
    masked_low = masked.astype(jnp.bfloat16)
    mixed = jnp.einsum(
        "hij,jhd->ihd",
        collide,
        masked_low.reshape(length, HEADS, head_dim),
        preferred_element_type=jnp.float32,
    ).reshape(length, model_width)
    normed, norm_back = jax.vjp(partial(head_norm, head_count=HEADS, head_dim=head_dim), mixed)
    context = (normed + depth_conv(masked, kernel_f, segment)).astype(jnp.bfloat16)
    attended = jnp.dot(context, w_out, preferred_element_type=jnp.float32) + b_out.astype(
        jnp.float32
    )
    first, first_back = jax.vjp(
        layer_norm,
        block_input.astype(jnp.float32) + attended,
        gain_attn.astype(jnp.float32),
        shift_attn.astype(jnp.float32),
    )
    first_low = first.astype(jnp.bfloat16)
    gathered = lax.all_gather(first_low, "tensor", axis=0, tiled=True)
    upper = jnp.dot(gathered, w_up, preferred_element_type=jnp.float32) + b_up.astype(jnp.float32)
    active_f, gelu_back = jax.vjp(gelu_exact, upper)
    active = active_f.astype(jnp.bfloat16)
    branch = lax.psum_scatter(
        jnp.dot(active, w_down, preferred_element_type=jnp.float32).astype(jnp.bfloat16),
        "tensor",
        scatter_dimension=0,
        tiled=True,
    ).astype(jnp.float32) + b_down.astype(jnp.float32)
    block_output, second_back = jax.vjp(
        layer_norm, first + branch, gain_ffn.astype(jnp.float32), shift_ffn.astype(jnp.float32)
    )
    grad_second, grad_gain_ffn, grad_shift_ffn = second_back(out_grad.astype(jnp.float32))
    branch_grad = grad_second.astype(jnp.bfloat16)
    grad_b_down = jnp.sum(branch_grad.astype(jnp.float32), axis=0)
    grad_rows_all = lax.all_gather(branch_grad, "tensor", axis=0, tiled=True)
    active_grad = dot_last(grad_rows_all, w_down)
    grad_w_down = dot_first(active, grad_rows_all)
    upper_grad = gelu_back(active_grad)[0].astype(jnp.bfloat16)
    grad_w_up = dot_first(gathered, upper_grad)
    grad_b_up = jnp.sum(upper_grad.astype(jnp.float32), axis=0)
    first_grad_ffn = lax.psum_scatter(
        dot_last(upper_grad, w_up).astype(jnp.bfloat16), "tensor", scatter_dimension=0, tiled=True
    ).astype(jnp.float32)
    first_grad = grad_second + first_grad_ffn
    resid_grad, grad_gain_attn, grad_shift_attn = first_back(first_grad)
    attended_grad = resid_grad.astype(jnp.bfloat16)
    grad_b_out = jnp.sum(attended_grad.astype(jnp.float32), axis=0)
    grad_w_out = dot_first(context, attended_grad)
    context_grad = dot_last(attended_grad, w_out)
    mixed_grad = norm_back(context_grad)[0].astype(jnp.bfloat16)
    conv_value_grad, grad_kernel = conv_back(context_grad, masked, kernel_f, segment)
    masked_att = jnp.einsum(
        "hij,ihd->jhd",
        collide,
        mixed_grad.reshape(length, HEADS, head_dim),
        preferred_element_type=jnp.float32,
    ).reshape(length, model_width)
    value_grad = ((masked_att + conv_value_grad) * live_keys).astype(jnp.bfloat16)
    grad_b_value = jnp.sum(value_grad.astype(jnp.float32), axis=0)
    grad_w_value = dot_first(block_input, value_grad)
    input_grad = resid_grad + dot_last(value_grad, w_value)
    grad_w_up, grad_w_down, grad_b_up = (
        lax.psum(grad_w_up.astype(jnp.bfloat16), "dp").astype(jnp.float32),
        lax.psum(grad_w_down.astype(jnp.bfloat16), "dp").astype(jnp.float32),
        lax.psum(grad_b_up.astype(jnp.bfloat16), "dp").astype(jnp.float32),
    )
    (
        grad_w_value,
        grad_b_value,
        grad_kernel,
        grad_w_out,
        grad_b_out,
        grad_gain_attn,
        grad_shift_attn,
        grad_b_down,
        grad_gain_ffn,
        grad_shift_ffn,
    ) = lax.psum(
        (
            grad_w_value,
            grad_b_value,
            grad_kernel,
            grad_w_out,
            grad_b_out,
            grad_gain_attn,
            grad_shift_attn,
            grad_b_down,
            grad_gain_ffn,
            grad_shift_ffn,
        ),
        ("dp", "tensor"),
    )
    return (
        block_output.astype(jnp.bfloat16),
        input_grad,
        grad_w_value,
        grad_b_value,
        grad_kernel,
        grad_w_out,
        grad_b_out,
        grad_gain_attn,
        grad_shift_attn,
        grad_w_up,
        grad_b_up,
        grad_w_down,
        grad_b_down,
        grad_gain_ffn,
        grad_shift_ffn,
    )


def solution(mesh):
    return jax.shard_map(
        body,
        mesh=mesh,
        in_specs=(
            P(("dp", "tensor"), None),
            P(),
            P(),
            P(),
            P(),
            P(),
            P(),
            P(),
            P(None, "tensor"),
            P("tensor"),
            P("tensor", None),
            P(),
            P(),
            P(),
            P(("dp", "tensor"), None),
            P(("dp", "tensor"), None),
            P(("dp", "tensor")),
            P(("dp", "tensor"), None),
            P(("dp", "tensor"), None),
        ),
        out_specs=(
            P(("dp", "tensor"), None),
            P(("dp", "tensor"), None),
            P(),
            P(),
            P(),
            P(),
            P(),
            P(),
            P(),
            P(None, "tensor"),
            P("tensor"),
            P("tensor", None),
            P(),
            P(),
            P(),
        ),
        check_vma=False,
    )
```

profile of v0, /device:TPU:1, one launch (start us, length us, event | category | flops | bytes accessed | tf_op | source)
XLA Modules:
  0.0 701.4 jit_solution(10940862884612107198)
XLA Ops:
  17.3 43.1 %while.12 = (s32[]{:T(128)}, bf16[12,256,256]{2,1,0:T(8,128)(2,1)}, s32[12,256,32]{1,2,0:T(8,128)S(1)}, s32[12,256,32]{1,2,0:T(8,128)S(1)}, s32[256]{0:T(256)S(1)}, /*index=5*/s32[]{:T(128)}) while((s32[]{:T(128)}, bf16[12,256,256]{2,1,0:T(8,128)(2,1)}, s32[12,256,32]{1,2,0:T(8,128)S(1)}, s32[12,256,32]{1,2,0:T(8,128)S(1)}, ...), condition=%wide.region_3.4_spmd.clone.clone, body=%wide.region_2.3_spmd.clone.clone.sunk | while | flops 1078198272 | bytes 330313 | solution.py:125
  17.4 3.6 fusion.266
  21.0 3.6 fusion.266
  24.6 3.6 fusion.266
  28.1 3.6 fusion.266
  31.7 3.6 fusion.266
  35.3 3.6 fusion.266
  38.9 3.6 fusion.266
  42.5 3.6 fusion.266
  46.1 3.6 fusion.266
  49.7 3.6 fusion.266
  53.3 3.6 fusion.266
  56.8 3.6 fusion.266
  61.2 2.0 multiply_reduce_fusion.70
  66.3 11.6 %add_convert_fusion.2 = bf16[256,768]{1,0:T(8,128)(2,1)S(1)} fusion(f32[256,768]{1,0:T(8,128)S(1)} %copy.51, f32[256,768]{1,0:T(8,128)S(1)} %get-tuple-element.368, f32[768]{0:T(1024)} %get-tuple-element.198, f32[256]{0:T(256)} %get-tuple-element.366, f32[768]{0:T(1024)} %get-tuple-element.199, f32[256]{0:T(256)} %get-tuple-element.365, ...), kind=kLoop, calls=%fused_computation.456 | loop fusion | flops 38338560 | bytes 2231296 | tf_op jit(solution)/shard_map/convert_element_type | solution.py:140
  78.7 1.9 fusion.236
  83.6 11.4 %reduce-scatter.3.cloned.1.call-start = ((), (), s32[]{:S(2)}) async-start(), calls=%async_computation.3 | async-start | bytes 3538944 | tf_op jit(solution)/shard_map/reduce_scatter | solution.py:155
  96.2 53.2 %all-gather.3.cloned.1.call-done = bf16[2048,768]{1,0:T(8,128)(2,1)} async-done(((bf16[256,768]{1,0:T(8,128)(2,1)}), bf16[2048,768]{1,0:T(8,128)(2,1)}) %all-gather.3.cloned.1.call-update) | async-done | bytes 3145744 | tf_op jit(solution)/shard_map/all_gather | solution.py:151
  149.4 11.6 %multiply_convert_fusion = (bf16[2048,384]{1,0:T(8,128)(2,1)S(1)}, f32[2048,384]{1,0:T(8,128)}, f32[2048,384]{1,0:T(8,128)}) fusion(f32[384]{0:T(512)} %convert_element_type.529, bf16[2048,768]{1,0:T(8,128)(2,1)} %all-gather.3.cloned.1.call-done, bf16[768,384]{1,0:T(8,128)(2,1)} %param.29), kind=kOutput, calls=%fused_computation.148 | convolution fusion | flops 1259864064 | bytes 11601408 | tf_op jit(solution)/shard_map/dot_general | solution.py:152
  162.2 3.4 convolution_convert_fusion.1
  169.5 72.7 %reduce-scatter.3.cloned.1.call-done = bf16[256,768]{1,0:T(8,128)(2,1)} async-done(((bf16[2048,768]{1,0:T(8,128)(2,1)}), bf16[256,768]{1,0:T(8,128)(2,1)}) %reduce-scatter.3.cloned.1.call-update) | async-done | bytes 393232 | tf_op jit(solution)/shard_map/reduce_scatter | solution.py:155
  243.9 1.9 fusion.26
  249.4 62.5 %all-gather.5.cloned.1.call-done = bf16[2048,768]{1,0:T(8,128)(2,1)} async-done(((bf16[256,768]{1,0:T(8,128)(2,1)}), bf16[2048,768]{1,0:T(8,128)(2,1)}) %all-gather.5.cloned.1.call-update) | async-done | bytes 3145744 | tf_op jit(solution)/shard_map/all_gather | solution.py:167
  311.9 7.3 %fusion.230 = (bf16[384]{0:T(512)(128)(2,1)}, bf16[2048,384]{1,0:T(8,128)(2,1)S(1)}) fusion(f32[2048,384]{1,0:T(8,128)} %get-tuple-element.299, f32[2048,384]{1,0:T(8,128)} %get-tuple-element.373, bf16[2048,768]{1,0:T(8,128)(2,1)} %all-gather.5.cloned.1.call-done, bf16[384,768]{1,0:T(8,128)(2,1)} %param.31), kind=kOutput, calls=%fused_computation.674 | convolution fusion | flops 1219755648 | bytes 11600640 | tf_op jit(solution)/shard_map/dot_general | solution.py:13
  320.4 3.5 convolution_convert_fusion
  324.0 4.8 convolution_convert_fusion.2
  328.8 2.6 convolution_convert_fusion.3
  331.5 69.1 %reduce-scatter.5.cloned.1.call-done = bf16[256,768]{1,0:T(8,128)(2,1)} async-done(((bf16[2048,768]{1,0:T(8,128)(2,1)}), bf16[256,768]{1,0:T(8,128)(2,1)}) %reduce-scatter.5.cloned.1.call-update) | async-done | bytes 393232 | tf_op jit(solution)/shard_map/reduce_scatter | solution.py:173
  400.6 2.4 multiply_reduce_fusion
  407.5 1.9 fusion.237
  410.8 3.0 multiply_reduce_fusion.46
  413.8 2.9 multiply_reduce_fusion.37
  416.8 2.1 multiply_reduce_fusion.19
  419.0 2.1 multiply_reduce_fusion.10
  421.3 2.9 multiply_reduce_fusion.1
  424.3 2.1 multiply_reduce_fusion.28
  426.5 2.2 multiply_reduce_fusion.55
  451.9 5.8 stack.263
  457.7 11.7 %convert_reduce_fusion.3 = (f32[768]{0:T(1024)S(1)}, bf16[256,768]{1,0:T(8,128)(2,1)S(1)}) fusion(f32[256]{0:T(256)} %copy-done.110, f32[256,768]{1,0:T(8,128)S(1)} %copy.53, f32[768]{0:T(1024)} %get-tuple-element.198, f32[256]{0:T(256)} %get-tuple-element.303, f32[768]{0:T(1024)} %get-tuple-element.199, f32[256]{0:T(256)} %get-tuple-element.321, ...), kind=kLoop, calls=%fused_computation.446 | loop fusion | flops 38927616 | bytes 2235392 | tf_op jit(solution)/shard_map/reduce_sum | solution.py:191
  469.4 1.9 convolution_bitcast_fusion
  472.0 28.5 %psum.99 = bf16[384]{0:T(512)(128)(2,1)S(1)} all-reduce(bf16[384]{0:T(512)(128)(2,1)S(1)} %copy-done.120), channel_id=1, replica_groups=mesh['dp'=16,'tensor'=8] {'dp'}, use_global_device_ids=true, to_apply=%region_94.95 | all-reduce | flops 384 | bytes 1536 | tf_op jit(solution)/shard_map/psum | solution.py:197
  501.1 22.6 %all-reduce.11.cloned.1.call-done = (bf16[768,384]{1,0:T(8,128)(2,1)}, bf16[384,768]{1,0:T(8,128)(2,1)}) async-done(((bf16[768,384]{1,0:T(8,128)(2,1)}, bf16[384,768]{1,0:T(8,128)(2,1)}), (bf16[768,384]{1,0:T(8,128)(2,1)}, bf16[384,768]{1,0:T(8,128)(2,1)})) %all-reduce.11.cloned.1.call-update) | async-done | bytes 1179664 | tf_op jit(solution)/shard_map/psum | solution.py:195
  523.7 2.2 convert_element_type.548
  525.9 2.2 convert_element_type.551
  528.0 68.4 %all-reduce.3 = (f32[768]{0:T(1024)}, f32[768]{0:T(1024)}, f32[768]{0:T(1024)}, f32[768]{0:T(1024)}, f32[768]{0:T(1024)}, /*index=5*/f32[768]{0:T(1024)}, f32[768]{0:T(1024)}) all-reduce(f32[768]{0:T(1024)S(1)} %get-tuple-element.290, f32[768]{0:T(1024)S(1)} %copy-done.37, ...), channel_id=1, replica_groups=mesh['dp'=16,'tensor'=8] {'dp','tensor'}, use_global_device_ids=true, to_apply=%region_18.19 | all-reduce | flops 5376 | bytes 43008 | tf_op jit(solution)/shard_map/psum | solution.py:210
  597.9 89.3 %all-reduce.9.cloned.1.call-done = (f32[768,768]{0,1:T(8,128)}, f32[65,768]{1,0:T(8,128)}, f32[768,768]{1,0:T(8,128)}) async-done(((f32[768,768]{0,1:T(8,128)}, f32[65,768]{1,0:T(8,128)}, f32[768,768]{1,0:T(8,128)}), (f32[768,768]{0,1:T(8,128)}, f32[65,768]{1,0:T(8,128)}, f32[768,768]{1,0:T(8,128)})) %all-reduce.9.cloned.1.call-update) | async-done | bytes 4918288 | tf_op jit(solution)/shard_map/psum | solution.py:210
  687.1 3.1 copy.54
  690.9 3.2 copy.70
  (389 shorter events, 61.7 us)
Async XLA Ops:
  7.2 53.3 %copy-start = (bf16[768,768]{1,0:T(8,128)(2,1)S(1)}, bf16[768,768]{1,0:T(8,128)(2,1)}, u32[]{:S(2)}) copy-start(bf16[768,768]{1,0:T(8,128)(2,1)} %param.22) | copy-start | bytes 3538948
  7.2 142.2 %all-gather.3.cloned.1.call-start = ((), (), s32[]{:S(2)}) async-start(), calls=%async_computation.2 | async-start | bytes 3538944 | tf_op jit(solution)/shard_map/all_gather | solution.py:151
  17.3 43.1 %copy-start.119 = (s32[256]{0:T(256)S(1)}, s32[256]{0:T(256)}, u32[]{:S(2)}) copy-start(s32[256]{0:T(256)} %param.37) | copy-start | bytes 3076
  17.3 43.1 %copy-start.116 = (bf16[768]{0:T(1024)(128)(2,1)S(1)}, bf16[768]{0:T(1024)(128)(2,1)}, u32[]{:S(2)}) copy-start(bf16[768]{0:T(1024)(128)(2,1)} %param.23) | copy-start | bytes 4612
  17.3 43.1 %copy-start.6 = (bf16[256,768]{1,0:T(8,128)(2,1)S(1)}, bf16[256,768]{1,0:T(8,128)(2,1)}, u32[]{:S(2)}) copy-start(bf16[256,768]{1,0:T(8,128)(2,1)} %param.21) | copy-start | bytes 1179652
  83.6 158.7 %reduce-scatter.3.cloned.1.call-start = ((), (), s32[]{:S(2)}) async-start(), calls=%async_computation.3 | async-start | bytes 3538944 | tf_op jit(solution)/shard_map/reduce_scatter | solution.py:155
  165.6 146.3 %all-gather.5.cloned.1.call-start = ((), (), s32[]{:S(2)}) async-start(), calls=%async_computation.4 | async-start | bytes 3538944 | tf_op jit(solution)/shard_map/all_gather | solution.py:167
  249.3 151.3 %reduce-scatter.5.cloned.1.call-start = ((), (), s32[]{:S(2)}) async-start(), calls=%async_computation.5 | async-start | bytes 3538944 | tf_op jit(solution)/shard_map/reduce_scatter | solution.py:173
  323.9 199.8 %all-reduce.11.cloned.1.call-start = ((), (), s32[]{:S(2)}) async-start(), calls=%async_computation.7 | async-start | bytes 2359296 | tf_op jit(solution)/shard_map/psum | solution.py:195
  331.4 355.7 %all-reduce.9.cloned.1.call-start = ((), (), s32[]{:S(2)}) async-start(), calls=%async_computation.6 | async-start | bytes 9879552 | tf_op jit(solution)/shard_map/psum | solution.py:210
  428.9 20.9 %copy-start.66 = (f32[768]{0:T(1024)S(1)}, f32[768]{0:T(1024)}, u32[]{:S(2)}) copy-start(f32[768]{0:T(1024)} %get-tuple-element.138) | copy-start | bytes 9220
  428.9 21.0 %copy-start.65 = (f32[768]{0:T(1024)S(1)}, f32[768]{0:T(1024)}, u32[]{:S(2)}) copy-start(f32[768]{0:T(1024)} %get-tuple-element.137) | copy-start | bytes 9220
  429.0 21.0 %copy-start.64 = (f32[768]{0:T(1024)S(1)}, f32[768]{0:T(1024)}, u32[]{:S(2)}) copy-start(f32[768]{0:T(1024)} %get-tuple-element.136) | copy-start | bytes 9220
  429.0 21.0 %copy-start.63 = (f32[768]{0:T(1024)S(1)}, f32[768]{0:T(1024)}, u32[]{:S(2)}) copy-start(f32[768]{0:T(1024)} %get-tuple-element.135) | copy-start | bytes 9220
  429.0 21.0 %copy-start.62 = (f32[768]{0:T(1024)S(1)}, f32[768]{0:T(1024)}, u32[]{:S(2)}) copy-start(f32[768]{0:T(1024)} %get-tuple-element.134) | copy-start | bytes 9220
  429.0 21.0 %copy-start.61 = (f32[768]{0:T(1024)S(1)}, f32[768]{0:T(1024)}, u32[]{:S(2)}) copy-start(f32[768]{0:T(1024)} %get-tuple-element.133) | copy-start | bytes 9220
  429.0 21.0 %copy-start.60 = (f32[768]{0:T(1024)S(1)}, f32[768]{0:T(1024)}, u32[]{:S(2)}) copy-start(f32[768]{0:T(1024)} %get-tuple-element.132) | copy-start | bytes 9220
  429.0 21.0 %copy-start.59 = (f32[768]{0:T(1024)S(1)}, f32[768]{0:T(1024)}, u32[]{:S(2)}) copy-start(f32[768]{0:T(1024)} %get-tuple-element.131) | copy-start | bytes 9220
  429.0 21.0 %copy-start.58 = (f32[768]{0:T(1024)S(1)}, f32[768]{0:T(1024)}, u32[]{:S(2)}) copy-start(f32[768]{0:T(1024)} %get-tuple-element.130) | copy-start | bytes 9220
  429.0 21.0 %copy-start.57 = (f32[768]{0:T(1024)S(1)}, f32[768]{0:T(1024)}, u32[]{:S(2)}) copy-start(f32[768]{0:T(1024)} %get-tuple-element.129) | copy-start | bytes 9220
  429.0 21.1 %copy-start.56 = (f32[768]{0:T(1024)S(1)}, f32[768]{0:T(1024)}, u32[]{:S(2)}) copy-start(f32[768]{0:T(1024)} %get-tuple-element.128) | copy-start | bytes 9220
  429.0 21.1 %copy-start.55 = (f32[768]{0:T(1024)S(1)}, f32[768]{0:T(1024)}, u32[]{:S(2)}) copy-start(f32[768]{0:T(1024)} %get-tuple-element.163) | copy-start | bytes 9220
  429.1 21.1 %copy-start.54 = (f32[768]{0:T(1024)S(1)}, f32[768]{0:T(1024)}, u32[]{:S(2)}) copy-start(f32[768]{0:T(1024)} %get-tuple-element.162) | copy-start | bytes 9220
  429.1 21.1 %copy-start.53 = (f32[768]{0:T(1024)S(1)}, f32[768]{0:T(1024)}, u32[]{:S(2)}) copy-start(f32[768]{0:T(1024)} %get-tuple-element.161) | copy-start | bytes 9220
  429.1 21.1 %copy-start.52 = (f32[768]{0:T(1024)S(1)}, f32[768]{0:T(1024)}, u32[]{:S(2)}) copy-start(f32[768]{0:T(1024)} %get-tuple-element.160) | copy-start | bytes 9220
  429.1 21.1 %copy-start.51 = (f32[768]{0:T(1024)S(1)}, f32[768]{0:T(1024)}, u32[]{:S(2)}) copy-start(f32[768]{0:T(1024)} %get-tuple-element.159) | copy-start | bytes 9220
  429.1 21.1 %copy-start.50 = (f32[768]{0:T(1024)S(1)}, f32[768]{0:T(1024)}, u32[]{:S(2)}) copy-start(f32[768]{0:T(1024)} %get-tuple-element.158) | copy-start | bytes 9220
  429.1 21.1 %copy-start.49 = (f32[768]{0:T(1024)S(1)}, f32[768]{0:T(1024)}, u32[]{:S(2)}) copy-start(f32[768]{0:T(1024)} %get-tuple-element.157) | copy-start | bytes 9220
  429.1 21.2 %copy-start.48 = (f32[768]{0:T(1024)S(1)}, f32[768]{0:T(1024)}, u32[]{:S(2)}) copy-start(f32[768]{0:T(1024)} %get-tuple-element.156) | copy-start | bytes 9220
  429.1 21.2 %copy-start.47 = (f32[768]{0:T(1024)S(1)}, f32[768]{0:T(1024)}, u32[]{:S(2)}) copy-start(f32[768]{0:T(1024)} %get-tuple-element.155) | copy-start | bytes 9220
  429.1 21.2 %copy-start.46 = (f32[768]{0:T(1024)S(1)}, f32[768]{0:T(1024)}, u32[]{:S(2)}) copy-start(f32[768]{0:T(1024)} %get-tuple-element.190) | copy-start | bytes 9220
  429.1 21.2 %copy-start.45 = (f32[768]{0:T(1024)S(1)}, f32[768]{0:T(1024)}, u32[]{:S(2)}) copy-start(f32[768]{0:T(1024)} %get-tuple-element.189) | copy-start | bytes 9220
  429.2 21.2 %copy-start.44 = (f32[768]{0:T(1024)S(1)}, f32[768]{0:T(1024)}, u32[]{:S(2)}) copy-start(f32[768]{0:T(1024)} %get-tuple-element.188) | copy-start | bytes 9220
  429.2 21.2 %copy-start.43 = (f32[768]{0:T(1024)S(1)}, f32[768]{0:T(1024)}, u32[]{:S(2)}) copy-start(f32[768]{0:T(1024)} %get-tuple-element.187) | copy-start | bytes 9220
  429.2 21.2 %copy-start.42 = (f32[768]{0:T(1024)S(1)}, f32[768]{0:T(1024)}, u32[]{:S(2)}) copy-start(f32[768]{0:T(1024)} %get-tuple-element.186) | copy-start | bytes 9220
  429.2 21.2 %copy-start.41 = (f32[768]{0:T(1024)S(1)}, f32[768]{0:T(1024)}, u32[]{:S(2)}) copy-start(f32[768]{0:T(1024)} %get-tuple-element.185) | copy-start | bytes 9220
  429.2 21.3 %copy-start.40 = (f32[768]{0:T(1024)S(1)}, f32[768]{0:T(1024)}, u32[]{:S(2)}) copy-start(f32[768]{0:T(1024)} %get-tuple-element.184) | copy-start | bytes 9220
  429.2 21.3 %copy-start.39 = (f32[768]{0:T(1024)S(1)}, f32[768]{0:T(1024)}, u32[]{:S(2)}) copy-start(f32[768]{0:T(1024)} %get-tuple-element.183) | copy-start | bytes 9220
  429.2 21.3 %copy-start.38 = (f32[768]{0:T(1024)S(1)}, f32[768]{0:T(1024)}, u32[]{:S(2)}) copy-start(f32[768]{0:T(1024)} %get-tuple-element.182) | copy-start | bytes 9220
  430.6 38.8 %copy-start.7 = (bf16[256,768]{1,0:T(8,128)(2,1)S(1)}, bf16[256,768]{1,0:T(8,128)(2,1)}, u32[]{:S(2)}) copy-start(bf16[256,768]{1,0:T(8,128)(2,1)} %param.21) | copy-start | bytes 1179652
  471.3 56.7 %copy-start.32 = (f32[768]{0:T(1024)S(1)}, f32[768]{0:T(1024)}, u32[]{:S(2)}) copy-start(f32[768]{0:T(1024)} %get-tuple-element.193) | copy-start | bytes 9220
  471.3 56.7 %copy-start.33 = (f32[768]{0:T(1024)S(1)}, f32[768]{0:T(1024)}, u32[]{:S(2)}) copy-start(f32[768]{0:T(1024)} %get-tuple-element.196) | copy-start | bytes 9220
  471.3 56.7 %copy-start.34 = (f32[768]{0:T(1024)S(1)}, f32[768]{0:T(1024)}, u32[]{:S(2)}) copy-start(f32[768]{0:T(1024)} %get-tuple-element.286) | copy-start | bytes 9220
  471.3 56.7 %copy-start.35 = (f32[768]{0:T(1024)S(1)}, f32[768]{0:T(1024)}, u32[]{:S(2)}) copy-start(f32[768]{0:T(1024)} %get-tuple-element.126) | copy-start | bytes 9220
  471.3 56.7 %copy-start.36 = (f32[768]{0:T(1024)S(1)}, f32[768]{0:T(1024)}, u32[]{:S(2)}) copy-start(f32[768]{0:T(1024)} %get-tuple-element.195) | copy-start | bytes 9220
  471.4 56.7 %copy-start.37 = (f32[768]{0:T(1024)S(1)}, f32[768]{0:T(1024)}, u32[]{:S(2)}) copy-start(f32[768]{0:T(1024)} %get-tuple-element.288) | copy-start | bytes 9220
  471.4 125.1 %copy-start.3 = (f32[256,768]{1,0:T(8,128)S(1)}, f32[256,768]{1,0:T(8,128)}, u32[]{:S(2)}) copy-start(f32[256,768]{1,0:T(8,128)} %copy-done.2) | copy-start | bytes 2359300
  471.4 125.1 %copy-start.115 = (f32[256]{0:T(256)S(1)}, f32[256]{0:T(256)}, u32[]{:S(2)}) copy-start(f32[256]{0:T(256)} %copy-done.114) | copy-start | bytes 3076
  (82 other events, 654.4 us)
Sparse Core Ops, SparseCore 0:
  83.7 65.6 all-gather.2
  165.7 76.4 reduce-scatter.2
  249.5 62.4 all-gather.4
  324.0 76.5 reduce-scatter.4
  403.6 120.0 all-reduce.10
  529.7 157.4 all-reduce.8
where the time goes:
time: 710 us; the launch traced here: 701 us
  waiting for transfers between devices  369 us (52%)
  blocking collectives  97 us (14%)
  matrix products  88.4 us (12%)
  other arithmetic  70.4 us (10%)
  local copies, waits for them, and re-layouts  48.2 us (7%)
  between operations  16.4 us (2%)
  starting transfers between devices  11.6 us (2%)
    psum x1, waiting for transfers between devices, body(): lax.psum((grad_w_value, grad_b_value, grad_kernel, grad_w_out, grad_b_out...  89.3 us
    reduce_scatter x1, waiting for transfers between devices, body(): lax.psum_scatter(jnp.dot(active, w_down, preferred_element_type=jnp.float...  72.7 us
    reduce_scatter x1, waiting for transfers between devices, body(): lax.psum_scatter(dot_last(upper_grad, w_up).astype(jnp.bfloat16), 'tensor...  69.1 us
    psum x1, blocking collectives, body(): lax.psum((grad_w_value, grad_b_value, grad_kernel, grad_w_out, grad_b_out...  68.4 us
    all_gather x1, waiting for transfers between devices, body(): grad_rows_all = lax.all_gather(branch_grad, 'tensor', axis=0, tiled=True)  62.5 us
    dot_general x16, matrix products, dot_last(): lax.dot_general(former, latter, (((1,), (1,)), ((), ())), preferred_eleme...  56.4 us
    all_gather x1, waiting for transfers between devices, body(): gathered = lax.all_gather(first_low, 'tensor', axis=0, tiled=True)  53.2 us
    psum x1, blocking collectives, body(): lax.psum(grad_b_up.astype(jnp.bfloat16), 'dp').astype(jnp.float32)  28.5 us
  transfers between devices with their start and end apart: 6, of which 6 were waited for; matrix products, arithmetic and copies ran while one was open for 12% of the time, Pallas kernels for 0%

commit v1 on v0

--- a/solution.py
+++ b/solution.py
@@ -164,7 +164,9 @@
     grad_second, grad_gain_ffn, grad_shift_ffn = second_back(out_grad.astype(jnp.float32))
     branch_grad = grad_second.astype(jnp.bfloat16)
     grad_b_down = jnp.sum(branch_grad.astype(jnp.float32), axis=0)
-    grad_rows_all = lax.all_gather(branch_grad, "tensor", axis=0, tiled=True)
+    grad_rows_all = jnp.concatenate(
+        lax.all_to_all(jnp.stack([branch_grad] * lax.axis_size("tensor")), "tensor", 0, 0), axis=0
+    )
     active_grad = dot_last(grad_rows_all, w_down)
     grad_w_down = dot_first(active, grad_rows_all)
     upper_grad = gelu_back(active_grad)[0].astype(jnp.bfloat16)

time: 710 us -> 690 us (0.972)
  waiting for transfers between devices: 369 us -> 268 us
  local copies, waits for them, and re-layouts: 48.2 us -> 91.6 us
  blocking collectives: 97 us -> 133 us
    all_gather x1 -> x0, waiting for transfers between devices: 62.5 us -> none  [body(): grad_rows_all = lax.all_gather(branch_grad, 'tensor', axis=0, tiled=True)]
    another operation x66, local copies, waits for them, and re-layouts: 25 us -> 68.8 us  [conv_back(): return (value_grad, jnp.stack(tap_rows, axis=0))]
    all_to_all x0 -> x1, blocking collectives: none -> 39.9 us  [body(): lax.all_to_all(jnp.stack([branch_grad] * lax.axis_size('tensor')), 'tenso...]
    psum x1, waiting for transfers between devices: 22.6 us -> 0.01 us  [body(): lax.psum(grad_w_up.astype(jnp.bfloat16), 'dp').astype(jnp.float32)]
    psum x1, waiting for transfers between devices: 89.3 us -> 69.9 us  [body(): lax.psum((grad_w_value, grad_b_value, grad_kernel, grad_w_out, grad_b_out...]
    unnamed x253 -> x263, local copies, waits for them, and re-layouts: 16.1 us -> 15.4 us
  transfers between devices with their start and end apart: 6 -> 5, of which waited for: 6 -> 4; matrix products, arithmetic and copies ran while one was open for 12% -> 19% of each run, Pallas kernels for 0% -> 0%
where the time goes in v1:
time: 690 us; the launch traced here: 681 us
  waiting for transfers between devices  268 us (39%)
  blocking collectives  133 us (19%)
  local copies, waits for them, and re-layouts  91.6 us (13%)
  matrix products  86.6 us (13%)
  other arithmetic  74.5 us (11%)
  between operations  15.6 us (2%)
  starting transfers between devices  11.4 us (2%)
    reduce_scatter x1, waiting for transfers between devices, body(): lax.psum_scatter(jnp.dot(active, w_down, preferred_element_type=jnp.float...  72.8 us
    reduce_scatter x1, waiting for transfers between devices, body(): lax.psum_scatter(dot_last(upper_grad, w_up).astype(jnp.bfloat16), 'tensor...  72.1 us
    psum x1, waiting for transfers between devices, body(): lax.psum((grad_w_value, grad_b_value, grad_kernel, grad_w_out, grad_b_out...  69.9 us
    another operation x66, local copies, waits for them, and re-layouts, conv_back(): return (value_grad, jnp.stack(tap_rows, axis=0))  68.8 us
    psum x1, blocking collectives, body(): lax.psum((grad_w_value, grad_b_value, grad_kernel, grad_w_out, grad_b_out...  65.3 us
    all_gather x1, waiting for transfers between devices, body(): gathered = lax.all_gather(first_low, 'tensor', axis=0, tiled=True)  53.3 us
    dot_general x16, matrix products, dot_last(): lax.dot_general(former, latter, (((1,), (1,)), ((), ())), preferred_eleme...  52.4 us
    all_to_all x1, blocking collectives, body(): lax.all_to_all(jnp.stack([branch_grad] * lax.axis_size('tensor')), 'tenso...  39.9 us
  transfers between devices with their start and end apart: 5, of which 4 were waited for; matrix products, arithmetic and copies ran while one was open for 19% of the time, Pallas kernels for 0%

profile of v1, /device:TPU:1, one launch (start us, length us, event | category | flops | bytes accessed | tf_op | source)
XLA Modules:
  0.0 681.4 jit_solution(15733315069290165663)
XLA Ops:
  24.1 43.1 %while.12 = (s32[]{:T(128)}, bf16[12,256,256]{2,1,0:T(8,128)(2,1)}, s32[12,256,32]{1,2,0:T(8,128)S(1)}, s32[12,256,32]{1,2,0:T(8,128)S(1)}, s32[256]{0:T(256)S(1)}, /*index=5*/s32[]{:T(128)}) while((s32[]{:T(128)}, bf16[12,256,256]{2,1,0:T(8,128)(2,1)}, s32[12,256,32]{1,2,0:T(8,128)S(1)}, s32[12,256,32]{1,2,0:T(8,128)S(1)}, ...), condition=%wide.region_3.4_spmd.clone.clone, body=%wide.region_2.3_spmd.clone.clone.sunk | while | flops 1078198272 | bytes 329813 | solution.py:125
  24.2 3.6 fusion.266
  27.8 3.6 fusion.266
  31.4 3.6 fusion.266
  34.9 3.6 fusion.266
  38.5 3.6 fusion.266
  42.1 3.6 fusion.266
  45.7 3.6 fusion.266
  49.3 3.6 fusion.266
  52.9 3.6 fusion.266
  56.5 3.6 fusion.266
  60.1 3.6 fusion.266
  63.6 3.6 fusion.266
  67.2 2.0 multiply_reduce_fusion.70
  71.6 12.1 %add_convert_fusion.2 = bf16[256,768]{1,0:T(8,128)(2,1)S(1)} fusion(f32[256,768]{1,0:T(8,128)S(1)} %copy.51, f32[256,768]{1,0:T(8,128)S(1)} %get-tuple-element.368, f32[768]{0:T(1024)} %get-tuple-element.198, f32[256]{0:T(256)} %get-tuple-element.366, f32[768]{0:T(1024)} %get-tuple-element.199, f32[256]{0:T(256)} %get-tuple-element.365, ...), kind=kLoop, calls=%fused_computation.456 | loop fusion | flops 38338560 | bytes 2231296 | tf_op jit(solution)/shard_map/convert_element_type | solution.py:140
  84.5 1.9 fusion.236
  88.8 11.2 %reduce-scatter.3.cloned.1.call-start = ((), (), s32[]{:S(2)}) async-start(), calls=%async_computation.4 | async-start | bytes 3538944 | tf_op jit(solution)/shard_map/reduce_scatter | solution.py:155
  101.3 53.3 %all-gather.2.cloned.1.call-done = bf16[2048,768]{1,0:T(8,128)(2,1)} async-done(((bf16[256,768]{1,0:T(8,128)(2,1)}), bf16[2048,768]{1,0:T(8,128)(2,1)}) %all-gather.2.cloned.1.call-update) | async-done | bytes 3145744 | tf_op jit(solution)/shard_map/all_gather | solution.py:151
  154.6 11.6 %multiply_convert_fusion = (bf16[2048,384]{1,0:T(8,128)(2,1)S(1)}, f32[2048,384]{1,0:T(8,128)}, f32[2048,384]{1,0:T(8,128)}) fusion(f32[384]{0:T(512)} %convert_element_type.529, bf16[2048,768]{1,0:T(8,128)(2,1)} %all-gather.2.cloned.1.call-done, bf16[768,384]{1,0:T(8,128)(2,1)} %param.29), kind=kOutput, calls=%fused_computation.148 | convolution fusion | flops 1259864064 | bytes 11601408 | tf_op jit(solution)/shard_map/dot_general | solution.py:152
  167.4 3.4 convolution_convert_fusion.1
  174.7 72.8 %reduce-scatter.3.cloned.1.call-done = bf16[256,768]{1,0:T(8,128)(2,1)} async-done(((bf16[2048,768]{1,0:T(8,128)(2,1)}), bf16[256,768]{1,0:T(8,128)(2,1)}) %reduce-scatter.3.cloned.1.call-update) | async-done | bytes 393232 | tf_op jit(solution)/shard_map/reduce_scatter | solution.py:155
  249.1 1.9 fusion.26
  253.3 39.9 %all_to_all.5 = bf16[8,256,768]{2,1,0:T(8,128)(2,1)S(1)} all-to-all(bf16[8,256,768]{2,1,0:T(8,128)(2,1)S(1)} %stack.209), channel_id=1, replica_groups=mesh['dp'=16,'tensor'=8] {'tensor'}, dimensions={0} | all-to-all | bytes 6291456 | tf_op jit(solution)/shard_map/all_to_all | solution.py:168
  293.3 3.3 fusion.230
  297.8 3.5 convolution_convert_fusion
  301.4 4.7 convolution_convert_fusion.2
  306.2 2.6 convolution_convert_fusion.3
  308.9 72.1 %reduce-scatter.5.cloned.1.call-done = bf16[256,768]{1,0:T(8,128)(2,1)} async-done(((bf16[2048,768]{1,0:T(8,128)(2,1)}), bf16[256,768]{1,0:T(8,128)(2,1)}) %reduce-scatter.5.cloned.1.call-update) | async-done | bytes 393232 | tf_op jit(solution)/shard_map/reduce_scatter | solution.py:175
  381.0 2.4 multiply_reduce_fusion
  388.8 2.3 multiply_reduce_fusion.19
  391.3 2.7 multiply_reduce_fusion.55
  394.2 2.8 multiply_reduce_fusion.37
  397.0 2.9 multiply_reduce_fusion.46
  399.9 2.1 multiply_reduce_fusion.10
  402.1 2.1 multiply_reduce_fusion.28
  404.3 2.1 multiply_reduce_fusion.1
  407.0 3.2 fusion.237
  468.4 2.3 copy.53
  470.8 12.2 %stack.275 = f32[65,768]{1,0:T(8,128)} concatenate(f32[1,768]{1,0:T(1,128)} %stack.210, f32[1,768]{1,0:T(1,128)} %stack.211, f32[1,768]{1,0:T(1,128)} %stack.212, f32[1,768]{1,0:T(1,128)} %stack.213, f32[1,768]{1,0:T(1,128)} %stack.214, f32[1,768]{1,0:T(1,128)} %stack.215, f32[1,768]{1,0:T(1,128)} %stack.216, f32[1,768]{1,0:T(1,128)} %stack.217, f32[1,768]{1,0:T(1,128)} %stack.218, ...), dimensions={0} | concatenate | bytes 399360 | tf_op jit(solution)/shard_map/stack | solution.py:72
  483.0 12.0 %convert_reduce_fusion.3 = (f32[768]{0:T(1024)S(1)}, bf16[256,768]{1,0:T(8,128)(2,1)S(1)}) fusion(f32[256]{0:T(256)} %copy-done.116, f32[256,768]{1,0:T(8,128)} %copy.53, f32[768]{0:T(1024)} %get-tuple-element.198, f32[256]{0:T(256)} %get-tuple-element.303, f32[768]{0:T(1024)} %get-tuple-element.199, f32[256]{0:T(256)} %get-tuple-element.321, ...), kind=kLoop, calls=%fused_computation.446 | loop fusion | flops 38927616 | bytes 2235392 | tf_op jit(solution)/shard_map/reduce_sum | solution.py:193
  495.0 1.9 convolution_bitcast_fusion
  497.6 28.3 %psum.99 = bf16[384]{0:T(512)(128)(2,1)S(1)} all-reduce(bf16[384]{0:T(512)(128)(2,1)S(1)} %copy-done.122), channel_id=1, replica_groups=mesh['dp'=16,'tensor'=8] {'dp'}, use_global_device_ids=true, to_apply=%region_94.95 | all-reduce | flops 384 | bytes 1536 | tf_op jit(solution)/shard_map/psum | solution.py:199
  526.4 2.2 convert_element_type.548
  528.6 2.2 convert_element_type.551
  530.8 65.3 %all-reduce.3 = (f32[768]{0:T(1024)}, f32[768]{0:T(1024)}, f32[768]{0:T(1024)}, f32[768]{0:T(1024)}, f32[768]{0:T(1024)}, /*index=5*/f32[768]{0:T(1024)}, f32[768]{0:T(1024)}) all-reduce(f32[768]{0:T(1024)S(1)} %get-tuple-element.290, f32[768]{0:T(1024)S(1)} %copy-done.36, ...), channel_id=1, replica_groups=mesh['dp'=16,'tensor'=8] {'dp','tensor'}, use_global_device_ids=true, to_apply=%region_18.19 | all-reduce | flops 5376 | bytes 43008 | tf_op jit(solution)/shard_map/psum | solution.py:212
  597.5 69.9 %all-reduce.9.cloned.1.call-done = (f32[768,768]{0,1:T(8,128)}, f32[65,768]{1,0:T(8,128)}, f32[768,768]{1,0:T(8,128)}) async-done(((f32[768,768]{0,1:T(8,128)}, f32[65,768]{1,0:T(8,128)}, f32[768,768]{1,0:T(8,128)}), (f32[768,768]{0,1:T(8,128)}, f32[65,768]{1,0:T(8,128)}, f32[768,768]{1,0:T(8,128)})) %all-reduce.9.cloned.1.call-update) | async-done | bytes 4918288 | tf_op jit(solution)/shard_map/psum | solution.py:212
  667.4 3.1 copy.54
  671.2 3.2 copy.70
  (398 shorter events, 101.0 us)
Async XLA Ops:
  7.2 147.4 %all-gather.2.cloned.1.call-start = ((), (), s32[]{:S(2)}) async-start(), calls=%async_computation.3 | async-start | bytes 3538944 | tf_op jit(solution)/shard_map/all_gather | solution.py:151
  88.8 158.7 %reduce-scatter.3.cloned.1.call-start = ((), (), s32[]{:S(2)}) async-start(), calls=%async_computation.4 | async-start | bytes 3538944 | tf_op jit(solution)/shard_map/reduce_scatter | solution.py:155
  170.9 210.1 %reduce-scatter.5.cloned.1.call-start = ((), (), s32[]{:S(2)}) async-start(), calls=%async_computation.5 | async-start | bytes 3538944 | tf_op jit(solution)/shard_map/reduce_scatter | solution.py:175
  253.1 40.2 %copy-start.128 = (f32[2048,384]{1,0:T(8,128)S(1)}, f32[2048,384]{1,0:T(8,128)}, u32[]{:S(2)}) copy-start(f32[2048,384]{1,0:T(8,128)} %get-tuple-element.373) | copy-start | bytes 9437188
  253.3 39.9 %copy-start.124 = (bf16[384,768]{1,0:T(8,128)(2,1)S(1)}, bf16[384,768]{1,0:T(8,128)(2,1)}, u32[]{:S(2)}) copy-start(bf16[384,768]{1,0:T(8,128)(2,1)} %param.31) | copy-start | bytes 1769476
  253.3 39.9 %copy-start.127 = (f32[2048,384]{1,0:T(8,128)S(1)}, f32[2048,384]{1,0:T(8,128)}, u32[]{:S(2)}) copy-start(f32[2048,384]{1,0:T(8,128)} %get-tuple-element.299) | copy-start | bytes 9437188
  301.3 225.1 %all-reduce.11.cloned.1.call-start = ((), (), s32[]{:S(2)}) async-start(), calls=%async_computation.7 | async-start | bytes 2359296 | tf_op jit(solution)/shard_map/psum | solution.py:197
  308.8 358.6 %all-reduce.9.cloned.1.call-start = ((), (), s32[]{:S(2)}) async-start(), calls=%async_computation.6 | async-start | bytes 9879552 | tf_op jit(solution)/shard_map/psum | solution.py:212
  406.6 38.9 %copy-start.72 = (f32[768]{0:T(1024)S(1)}, f32[768]{0:T(1024)}, u32[]{:S(2)}) copy-start(f32[768]{0:T(1024)} %get-tuple-element.173) | copy-start | bytes 9220
  406.6 39.5 %copy-start.71 = (f32[768]{0:T(1024)S(1)}, f32[768]{0:T(1024)}, u32[]{:S(2)}) copy-start(f32[768]{0:T(1024)} %get-tuple-element.174) | copy-start | bytes 9220
  406.7 40.1 %copy-start.70 = (f32[768]{0:T(1024)S(1)}, f32[768]{0:T(1024)}, u32[]{:S(2)}) copy-start(f32[768]{0:T(1024)} %get-tuple-element.175) | copy-start | bytes 9220
  406.7 40.7 %copy-start.69 = (f32[768]{0:T(1024)S(1)}, f32[768]{0:T(1024)}, u32[]{:S(2)}) copy-start(f32[768]{0:T(1024)} %get-tuple-element.176) | copy-start | bytes 9220
  406.7 41.3 %copy-start.68 = (f32[768]{0:T(1024)S(1)}, f32[768]{0:T(1024)}, u32[]{:S(2)}) copy-start(f32[768]{0:T(1024)} %get-tuple-element.177) | copy-start | bytes 9220
  406.7 41.9 %copy-start.67 = (f32[768]{0:T(1024)S(1)}, f32[768]{0:T(1024)}, u32[]{:S(2)}) copy-start(f32[768]{0:T(1024)} %get-tuple-element.178) | copy-start | bytes 9220
  406.7 42.5 %copy-start.66 = (f32[768]{0:T(1024)S(1)}, f32[768]{0:T(1024)}, u32[]{:S(2)}) copy-start(f32[768]{0:T(1024)} %get-tuple-element.179) | copy-start | bytes 9220
  406.7 43.0 %copy-start.65 = (f32[768]{0:T(1024)S(1)}, f32[768]{0:T(1024)}, u32[]{:S(2)}) copy-start(f32[768]{0:T(1024)} %get-tuple-element.180) | copy-start | bytes 9220
  406.7 43.6 %copy-start.63 = (f32[768]{0:T(1024)S(1)}, f32[768]{0:T(1024)}, u32[]{:S(2)}) copy-start(f32[768]{0:T(1024)} %get-tuple-element.181) | copy-start | bytes 9220
  406.7 44.2 %copy-start.62 = (f32[768]{0:T(1024)S(1)}, f32[768]{0:T(1024)}, u32[]{:S(2)}) copy-start(f32[768]{0:T(1024)} %get-tuple-element.137) | copy-start | bytes 9220
  406.7 44.8 %copy-start.61 = (f32[768]{0:T(1024)S(1)}, f32[768]{0:T(1024)}, u32[]{:S(2)}) copy-start(f32[768]{0:T(1024)} %get-tuple-element.138) | copy-start | bytes 9220
  406.7 45.4 %copy-start.60 = (f32[768]{0:T(1024)S(1)}, f32[768]{0:T(1024)}, u32[]{:S(2)}) copy-start(f32[768]{0:T(1024)} %get-tuple-element.139) | copy-start | bytes 9220
  406.8 46.0 %copy-start.59 = (f32[768]{0:T(1024)S(1)}, f32[768]{0:T(1024)}, u32[]{:S(2)}) copy-start(f32[768]{0:T(1024)} %get-tuple-element.140) | copy-start | bytes 9220
  406.8 46.6 %copy-start.58 = (f32[768]{0:T(1024)S(1)}, f32[768]{0:T(1024)}, u32[]{:S(2)}) copy-start(f32[768]{0:T(1024)} %get-tuple-element.141) | copy-start | bytes 9220
  406.8 47.1 %copy-start.57 = (f32[768]{0:T(1024)S(1)}, f32[768]{0:T(1024)}, u32[]{:S(2)}) copy-start(f32[768]{0:T(1024)} %get-tuple-element.142) | copy-start | bytes 9220
  406.8 47.7 %copy-start.56 = (f32[768]{0:T(1024)S(1)}, f32[768]{0:T(1024)}, u32[]{:S(2)}) copy-start(f32[768]{0:T(1024)} %get-tuple-element.143) | copy-start | bytes 9220
  406.8 48.3 %copy-start.55 = (f32[768]{0:T(1024)S(1)}, f32[768]{0:T(1024)}, u32[]{:S(2)}) copy-start(f32[768]{0:T(1024)} %get-tuple-element.144) | copy-start | bytes 9220
  406.8 48.9 %copy-start.54 = (f32[768]{0:T(1024)S(1)}, f32[768]{0:T(1024)}, u32[]{:S(2)}) copy-start(f32[768]{0:T(1024)} %get-tuple-element.145) | copy-start | bytes 9220
  406.8 49.5 %copy-start.64 = (f32[768]{0:T(1024)S(1)}, f32[768]{0:T(1024)}, u32[]{:S(2)}) copy-start(f32[768]{0:T(1024)} %get-tuple-element.128) | copy-start | bytes 9220
  406.8 50.1 %copy-start.53 = (f32[768]{0:T(1024)S(1)}, f32[768]{0:T(1024)}, u32[]{:S(2)}) copy-start(f32[768]{0:T(1024)} %get-tuple-element.155) | copy-start | bytes 9220
  406.8 50.7 %copy-start.52 = (f32[768]{0:T(1024)S(1)}, f32[768]{0:T(1024)}, u32[]{:S(2)}) copy-start(f32[768]{0:T(1024)} %get-tuple-element.156) | copy-start | bytes 9220
  406.8 51.2 %copy-start.51 = (f32[768]{0:T(1024)S(1)}, f32[768]{0:T(1024)}, u32[]{:S(2)}) copy-start(f32[768]{0:T(1024)} %get-tuple-element.157) | copy-start | bytes 9220
  406.9 51.8 %copy-start.50 = (f32[768]{0:T(1024)S(1)}, f32[768]{0:T(1024)}, u32[]{:S(2)}) copy-start(f32[768]{0:T(1024)} %get-tuple-element.158) | copy-start | bytes 9220
  406.9 52.4 %copy-start.49 = (f32[768]{0:T(1024)S(1)}, f32[768]{0:T(1024)}, u32[]{:S(2)}) copy-start(f32[768]{0:T(1024)} %get-tuple-element.159) | copy-start | bytes 9220
  406.9 53.0 %copy-start.48 = (f32[768]{0:T(1024)S(1)}, f32[768]{0:T(1024)}, u32[]{:S(2)}) copy-start(f32[768]{0:T(1024)} %get-tuple-element.160) | copy-start | bytes 9220
  406.9 53.6 %copy-start.47 = (f32[768]{0:T(1024)S(1)}, f32[768]{0:T(1024)}, u32[]{:S(2)}) copy-start(f32[768]{0:T(1024)} %get-tuple-element.161) | copy-start | bytes 9220
  406.9 54.1 %copy-start.46 = (f32[768]{0:T(1024)S(1)}, f32[768]{0:T(1024)}, u32[]{:S(2)}) copy-start(f32[768]{0:T(1024)} %get-tuple-element.162) | copy-start | bytes 9220
  406.9 54.7 %copy-start.44 = (f32[768]{0:T(1024)S(1)}, f32[768]{0:T(1024)}, u32[]{:S(2)}) copy-start(f32[768]{0:T(1024)} %get-tuple-element.163) | copy-start | bytes 9220
  406.9 55.3 %copy-start.45 = (f32[768]{0:T(1024)S(1)}, f32[768]{0:T(1024)}, u32[]{:S(2)}) copy-start(f32[768]{0:T(1024)} %get-tuple-element.129) | copy-start | bytes 9220
  406.9 55.9 %copy-start.43 = (f32[768]{0:T(1024)S(1)}, f32[768]{0:T(1024)}, u32[]{:S(2)}) copy-start(f32[768]{0:T(1024)} %get-tuple-element.130) | copy-start | bytes 9220
  406.9 56.5 %copy-start.42 = (f32[768]{0:T(1024)S(1)}, f32[768]{0:T(1024)}, u32[]{:S(2)}) copy-start(f32[768]{0:T(1024)} %get-tuple-element.131) | copy-start | bytes 9220
  406.9 57.0 %copy-start.41 = (f32[768]{0:T(1024)S(1)}, f32[768]{0:T(1024)}, u32[]{:S(2)}) copy-start(f32[768]{0:T(1024)} %get-tuple-element.132) | copy-start | bytes 9220
  407.0 57.6 %copy-start.40 = (f32[768]{0:T(1024)S(1)}, f32[768]{0:T(1024)}, u32[]{:S(2)}) copy-start(f32[768]{0:T(1024)} %get-tuple-element.133) | copy-start | bytes 9220
  407.0 58.2 %copy-start.39 = (f32[768]{0:T(1024)S(1)}, f32[768]{0:T(1024)}, u32[]{:S(2)}) copy-start(f32[768]{0:T(1024)} %get-tuple-element.134) | copy-start | bytes 9220
  407.0 58.8 %copy-start.38 = (f32[768]{0:T(1024)S(1)}, f32[768]{0:T(1024)}, u32[]{:S(2)}) copy-start(f32[768]{0:T(1024)} %get-tuple-element.135) | copy-start | bytes 9220
  407.0 59.4 %copy-start.37 = (f32[768]{0:T(1024)S(1)}, f32[768]{0:T(1024)}, u32[]{:S(2)}) copy-start(f32[768]{0:T(1024)} %get-tuple-element.136) | copy-start | bytes 9220
  407.0 60.1 %copy-start.16 = (f32[256,12]{0,1:T(8,128)S(1)}, f32[256,12]{0,1:T(8,128)}, u32[]{:S(2)}) copy-start(f32[256,12]{0,1:T(8,128)} %copy-done.15) | copy-start | bytes 36868
  407.0 60.1 %copy-start.4 = (bf16[12,256,256]{2,1,0:T(8,128)(2,1)S(1)}, bf16[12,256,256]{2,1,0:T(8,128)(2,1)}, u32[]{:S(2)}) copy-start(bf16[12,256,256]{2,1,0:T(8,128)(2,1)} %get-tuple-element.50) | copy-start | bytes 4718596
  496.9 99.2 %copy-start.3 = (f32[256,768]{1,0:T(8,128)S(1)}, f32[256,768]{1,0:T(8,128)}, u32[]{:S(2)}) copy-start(f32[256,768]{1,0:T(8,128)} %copy-done.2) | copy-start | bytes 2359300
  496.9 99.2 %copy-start.121 = (f32[256]{0:T(256)S(1)}, f32[256]{0:T(256)}, u32[]{:S(2)}) copy-start(f32[256]{0:T(256)} %copy-done.120) | copy-start | bytes 3076
  (86 other events, 831.2 us)
Sparse Core Ops, SparseCore 0:
  88.9 65.6 all-gather.1
  171.0 76.4 reduce-scatter.2
  301.4 79.4 reduce-scatter.4
  383.9 120.1 all-reduce.10
  510.0 157.3 all-reduce.8
